TPU v7x, 128 devices: a whole 4x4x4 slice. The times are simulated.
128 devices in a mesh: row: 8 (over x, y_lo), col: 16 (over z, y_hi, core).
Axes of the slice: x: 4, y: 4 (y_hi: 2, y_lo: 2; y = y_hi * 2 + y_lo), z: 4, core: 2. Of those that a mesh axis runs over, the one named last changes fastest.
Arguments:
- elevation: float32 [4096, 16384], P('row', 'col'), may hold values from -6 to 6
- ocean: int32 [4096, 16384], P('row', 'col'), may hold values from 0 to 1, as said below
- outlet: int32 [4096, 16384], P('row', 'col'), may hold values from 0 to 1, as said below
Outputs:
- surface: float32 [4096, 16384], P('row', 'col')
Inputs may be any that keep to these rules, and one draw needn't show every extreme that they name: ocean cells are scattered; no bound on their count in any region may be assumed. outlet cells are scattered; no bound on their count in any region may be assumed.
All inputs are finite; a program needn't handle non-finite values.
Results may differ from a plain program's by a relative error of at most 0.00002.
Values sent between devices are 32-bit elements; how exact they have to be, the bound alone decides.
A program may use at most 128 MiB of HBM per device.

v0:
```python
import jax
import jax.numpy as jnp
from jax import lax
from jax.experimental import pallas as pl
from jax.experimental.pallas import tpu as pltpu
from jax.sharding import PartitionSpec as P

MESH = pl.DeviceIdType.MESH
HUGE = 1e30
FINE_STEP = 2.0 ** (-10)
COARSE_STEP = 2.0 ** (-6)
F32 = jnp.float32

K = 33
W = 144
A = 18

DIRS = [(-1, 0), (1, 0), (0, -1), (0, 1), (-1, -1), (-1, 1), (1, -1), (1, 1)]
N_, S_, W_, E_, NW_, NE_, SW_, SE_ = range(8)
OPP = [S_, N_, E_, W_, SE_, SW_, NE_, NW_]


def lanes():
    return lax.broadcasted_iota(jnp.int32, (8, 128), 1)


def subs():
    return lax.broadcasted_iota(jnp.int32, (8, 128), 0)


def merge(a, b, w, axis, pos, op):
    size = 8 if axis == 0 else 128
    low = (pos & w) == 0
    p = jnp.where(low, a, b)
    q = jnp.where(low, pltpu.roll(a, size - w, axis), pltpu.roll(b, w, axis))
    return op(p, q)


def tree(xs, ws, axis, pos, op):
    for w in ws:
        half = len(xs) // 2
        xs = [merge(xs[i], xs[i + half], w, axis, pos, op) for i in range(half)]
    return xs[0]


def neighbour(d, rows, cols):
    r = lax.axis_index("row")
    c = lax.axis_index("col")
    return (lax.rem(r + d[0] + rows, rows), lax.rem(c + d[1] + cols, cols))


def sweep(src, dst, g):
    def row(ref, k):
        return [ref[k, pl.ds(a, 8, stride=A), :] for a in range(A)]

    def across(vm):
        before = pltpu.roll(vm[A - 1], 1, 0)
        after = pltpu.roll(vm[0], 7, 0)
        m = [None] * A
        for a in range(0, A, 2):
            q = jnp.minimum(vm[a], vm[a + 1])
            m[a] = jnp.minimum(vm[a - 1] if a else before, q)
            m[a + 1] = jnp.minimum(q, vm[a + 2] if a + 2 < A else after)
        return m

    def put(k, v, m):
        out = []
        for a in range(A):
            x = jnp.maximum(g[k, pl.ds(a, 8, stride=A), :], jnp.minimum(v[a], m[a] + FINE_STEP))
            dst[k + 1, pl.ds(a, 8, stride=A), :] = x
            out.append(x)
        return out

    def pair(k):
        v0, v1, v2, v3 = (row(src, k + i) for i in range(4))
        p = [jnp.minimum(x, y) for x, y in zip(v1, v2)]
        m0 = across([jnp.minimum(x, y) for x, y in zip(v0, p)])
        m1 = across([jnp.minimum(x, y) for x, y in zip(p, v3)])
        return put(k, v1, m0), put(k + 1, v2, m1)

    v0, v1, v2 = (row(src, K - 1 + i) for i in range(3))
    last = put(K - 1, v1, across([jnp.minimum(jnp.minimum(x, y), z) for x, y, z in zip(v0, v1, v2)]))
    for a in range(A):
        dst[0, pl.ds(a, 8, stride=A), :] = pltpu.roll(last[a], 1, 1)
    first, _ = pair(0)
    for a in range(A):
        dst[K + 1, pl.ds(a, 8, stride=A), :] = pltpu.roll(first[a], 127, 1)

    def body(i, c):
        pair(2 + 2 * i)
        return c

    lax.fori_loop(0, (K - 3) // 2, body, 0)


def kernel(rows, cols, e_h, oc_h, ou_h, o_h, ev, ocv, ouv, gl, halo, tt, va, vb, ov, ca, cp, pk, cn, pwe, cf, zz,
           yy, xb, fs, fr, cs, cr, ht, in_sem, out_sem, send, recv):
    lane = lanes()
    sub = subs()
    north = lax.axis_index("row") == 0
    south = lax.axis_index("row") == rows - 1
    to = [neighbour(d, rows, cols) for d in DIRS]

    barrier = pltpu.get_barrier_semaphore()
    for dev in to:
        pl.semaphore_signal(barrier, inc=1, device_id=dev, device_id_type=MESH)

    def loads(j):
        at = pl.ds(128 * j, 128)
        return [pltpu.make_async_copy(h.at[:, at], v.at[j], in_sem.at[j, i])
                for i, (h, v) in enumerate(((e_h, ev), (oc_h, ocv), (ou_h, ouv)))]

    for j in range(8):
        for c in loads(j):
            c.start()

    for j in range(8):
        for c in loads(j):
            c.wait()

        def group(grp, carry, j=j):
            gmin, lmin, gmax = [], [], []
            for c in range(8):
                gs, ls = [], []
                for h in range(2):
                    r = pl.multiple_of(grp * 128 + 16 * c + 8 * h, 8)
                    oc = ocv[j, pl.ds(r, 8), :] == 1
                    ou = ouv[j, pl.ds(r, 8), :] == 1
                    g = jnp.where(oc, F32(0.0), ev[j, pl.ds(r, 8), :])
                    lk = jnp.where(oc | ou, g, F32(HUGE))
                    gl[0, j, pl.ds(r + 8, 8), :] = g
                    gl[1, j, pl.ds(r + 8, 8), :] = lk
                    gs.append(g)
                    ls.append(lk)
                gmin.append(jnp.minimum(*gs))
                lmin.append(jnp.minimum(*ls))
                gmax.append(jnp.maximum(*gs))
            at = pl.ds(pl.multiple_of(grp * 8, 8), 8)
            ca[0, j, at, :] = tree(gmin, (4, 2, 1), 0, sub, jnp.minimum)
            ca[1, j, at, :] = tree(lmin, (4, 2, 1), 0, sub, jnp.minimum)
            ca[2, j, at, :] = tree(gmax, (4, 2, 1), 0, sub, jnp.maximum)
            return carry

        lax.fori_loop(0, 4, group, 0)

    pl.semaphore_wait(barrier, 8)

    def copy(i, src, dst, d):
        return pltpu.make_async_remote_copy(src_ref=src, dst_ref=dst, send_sem=send.at[i], recv_sem=recv.at[i],
                                            device_id=to[d], device_id_type=MESH)

    copies = [None] * 16
    copies[N_] = copy(N_, gl.at[:, :, pl.ds(8, 8), :], halo.at[1], N_)
    copies[S_] = copy(S_, gl.at[:, :, pl.ds(512, 8), :], halo.at[0], S_)
    copies[N_].start()
    copies[S_].start()

    index = jnp.where((lane >= 8) & (lane < 72), 16 * ((lane - 8) & 7) + 2 * ((lane - 8) >> 3), 0)
    for a in range(3):
        op = jnp.maximum if a == 2 else jnp.minimum
        for grp in range(4):
            x = tree([ca[a, j, pl.ds(8 * grp, 8), :] for j in range(8)], (8, 4, 2), 1, lane, op)
            x = op(x, pltpu.roll(x, 127, 1))
            cp[a, pl.ds(8 * grp, 8), :] = jnp.take_along_axis(x, index, axis=1)
    for grp in range(4):
        at = pl.ds(8 * grp, 8)
        pk[at, :] = jnp.where(((lane >= 8) & (lane < 16)) | ((lane >= 64) & (lane < 72)), cp[0, at, :],
                              jnp.where(((lane >= 16) & (lane < 24)) | ((lane >= 72) & (lane < 80)),
                                        pltpu.roll(cp[1, at, :], 8, 1), pltpu.roll(cp[2, at, :], 16, 1)))
    top, bottom = pl.ds(0, 8), pl.ds(24, 8)
    copies[8 + N_] = copy(8 + N_, cp.at[:, top, :], cn.at[1], N_)
    copies[8 + S_] = copy(8 + S_, cp.at[:, bottom, :], cn.at[0], S_)
    copies[8 + W_] = copy(8 + W_, pk, pwe.at[1, pl.ds(8, 32), :], W_)
    copies[8 + E_] = copy(8 + E_, pk, pwe.at[0, pl.ds(8, 32), :], E_)
    copies[8 + NW_] = copy(8 + NW_, pk.at[top, :], pwe.at[1, pl.ds(40, 8), :], NW_)
    copies[8 + NE_] = copy(8 + NE_, pk.at[top, :], pwe.at[0, pl.ds(40, 8), :], NE_)
    copies[8 + SW_] = copy(8 + SW_, pk.at[bottom, :], pwe.at[1, pl.ds(0, 8), :], SW_)
    copies[8 + SE_] = copy(8 + SE_, pk.at[bottom, :], pwe.at[0, pl.ds(0, 8), :], SE_)
    for i in (NW_, NE_, SW_, SE_, W_, E_, N_, S_):
        copies[8 + i].start()

    for arr in range(2):
        for grp in range(5):
            parts = []
            for i in range(8):
                k = min(8 * grp + i, K - 1)
                for s in (0, 8):
                    at = pl.ds(k + K * s, 8, stride=K)
                    parts.append(jnp.where(lane < 64, gl[arr, 0, at, :], gl[arr, 7, at, :]))
            t = jnp.concatenate(parts, axis=0).T
            fs[0, arr, grp, :, :] = t[0:8, :]
            fs[1, arr, grp, :, :] = t[120:128, :]
        for side in range(2):
            cs[side, 0, arr, :, :] = pltpu.roll(fs[side, arr, 1, :, :], 31, 1)
            cs[side, 1, arr, :, :] = pltpu.roll(
                jnp.where(lane == 15, fs[side, arr, 3, :, :], fs[side, arr, 2, :, :]), 97, 1)
    copies[W_] = copy(W_, fs.at[0], fr.at[1], W_)
    copies[E_] = copy(E_, fs.at[1], fr.at[0], E_)
    copies[NW_] = copy(NW_, cs.at[0, 0], cr.at[1, 1], NW_)
    copies[NE_] = copy(NE_, cs.at[1, 0], cr.at[0, 1], NE_)
    copies[SW_] = copy(SW_, cs.at[0, 1], cr.at[1, 0], SW_)
    copies[SE_] = copy(SE_, cs.at[1, 1], cr.at[0, 0], SE_)
    for i in (NW_, NE_, SW_, SE_, W_, E_):
        copies[i].start()

    def turn(i, carry):
        for u in range(3):
            k = 3 * i + u
            for arr in range(2):
                parts = [gl[arr, j, pl.ds(k + K * s, 8, stride=K), :] for j in range(8) for s in (0, 8)]
                tt[arr, k, pl.ds(8, 128), :] = jnp.concatenate(parts, axis=0).T
        return carry

    lax.fori_loop(0, K // 3, turn, 0)

    for i in range(8):
        copies[i].wait()
    strip = lane & 15
    for arr in range(2):
        parts = []
        for j in range(8):
            parts.append(jnp.where(north, F32(HUGE), halo[0, arr, j, :, :]))
            parts.append(jnp.where(south, F32(HUGE), halo[1, arr, j, :, :]))
        ht[arr, :, :] = jnp.concatenate(parts, axis=0).T
    for arr in range(2):
        for k in range(8):
            for i in range(16):
                at = pl.ds(8 + 8 * i, 8)
                h = ht[arr, pl.ds(8 * i, 8), :]
                tt[arr, k, at, :] = jnp.where(strip == 0, pltpu.roll(h, (128 - k) % 128, 1), tt[arr, k, at, :])
                kk = k + 25
                tt[arr, kk, at, :] = jnp.where(strip == 15, pltpu.roll(h, 32 - kk, 1), tt[arr, kk, at, :])
        edge = []
        for side in range(2):
            up = jnp.where(north, F32(HUGE), cr[side, 0, arr, :, :])
            down = jnp.where(south, F32(HUGE), cr[side, 1, arr, :, :])
            e = [fr[side, arr, grp, :, :] for grp in range(5)]
            e[0] = jnp.where(strip == 0, up, e[0])
            e[3] = jnp.where((strip == 15) & (lane >= 31), down, e[3])
            e[4] = jnp.where(lane == 15, down, e[4])
            edge.append(e)
        for k in range(K):
            i = k % 8
            own = pltpu.roll(tt[arr, k, pl.ds(128, 8), :], 16, 1)
            got = pltpu.roll(edge[0][k // 8], (128 - 16 * i) % 128, 1)
            tt[arr, k, pl.ds(0, 8), :] = jnp.where(lane < 16, got, own)
            own = pltpu.roll(tt[arr, k, pl.ds(8, 8), :], 112, 1)
            got = pltpu.roll(edge[1][k // 8], (112 - 16 * i) % 128, 1)
            tt[arr, k, pl.ds(136, 8), :] = jnp.where(lane >= 112, got, own)

    for i in range(8):
        copies[8 + i].wait()
    ext = []
    for a in range(3):
        tiles = []
        for t in range(6):
            at = pl.ds(8 * t, 8)
            ring = pltpu.roll(jnp.where(lane < 64, pwe[1, at, :], pwe[0, at, :]), 64 - 8 * a, 1)
            mid = cn[0, a, :, :] if t == 0 else cn[1, a, :, :] if t == 5 else cp[a, pl.ds(8 * t - 8, 8), :]
            x = jnp.where((lane >= 8) & (lane < 72), mid, ring)
            if t == 0:
                x = jnp.where(north, F32(HUGE), x)
            if t == 5:
                x = jnp.where(south, F32(HUGE), x)
            tiles.append(x)
        ext.append(tiles)
    gc, kc, v = ext
    for _ in range(4):
        h = [jnp.minimum(jnp.minimum(pltpu.roll(x, 1, 1), pltpu.roll(x, 127, 1)), x) for x in v]
        up = [pltpu.roll(x, 1, 0) for x in h]
        down = [pltpu.roll(x, 7, 0) for x in h]
        new = []
        for t in range(6):
            u = jnp.where(sub == 0, up[t - 1], up[t])
            d = jnp.where(sub == 7, down[(t + 1) % 6], down[t])
            m = jnp.minimum(jnp.minimum(u, d), h[t])
            new.append(jnp.minimum(jnp.maximum(gc[t], jnp.minimum(v[t], m + COARSE_STEP)), kc[t]))
        v = new
    turned = jnp.concatenate(v + [v[0]] * 10, axis=0).T
    cf[...] = turned
    for d in range(4):
        idx = 2 * strip + 7 + d
        for t in range(10):
            at = pl.ds(8 * t, 8)
            zz[d, at, :] = jnp.take_along_axis(cf[at, :], idx, axis=1)
    for d in range(4):
        for t in range(2):
            y = zz[d, pl.ds(7 + 8 * t, 8), :]
            for j in range(1, 8):
                y = jnp.where((lane >> 4) == j, zz[d, pl.ds(7 + 8 * j + 8 * t, 8), :], y)
            yy[d, pl.ds(8 * t, 8), :] = y

    def begin(k, carry):
        d = (k + strip + 8) >> 4
        for t in range(2):
            at = pl.ds(8 * t, 8)
            xb[k, at, :] = jnp.where(d == 0, yy[0, at, :], jnp.where(d == 1, yy[1, at, :],
                                                                     jnp.where(d == 2, yy[2, at, :], yy[3, at, :])))
        return carry

    lax.fori_loop(0, K, begin, 0, unroll=3)

    def begin2(k, carry):
        for t in range(A):
            at = pl.ds(8 * t, 8)
            b = 0 if t == 0 else (t + 1) // 2
            x = xb[k, pl.ds(b, 8, stride=0), :]
            va[k + 1, at, :] = jnp.minimum(jnp.maximum(tt[0, k, at, :], x), tt[1, k, at, :])
        return carry

    lax.fori_loop(0, K, begin2, 0, unroll=3)
    for t in range(A):
        at = pl.ds(8 * t, 8)
        va[0, at, :] = pltpu.roll(va[K, at, :], 1, 1)
        va[K + 1, at, :] = pltpu.roll(va[1, at, :], 127, 1)

    def two(i, carry):
        sweep(va, vb, tt.at[0])
        sweep(vb, va, tt.at[0])
        return carry

    lax.fori_loop(0, 4, two, 0)

    def back(i, carry):
        for u in range(3):
            k = 3 * i + u
            t = va[k + 1, pl.ds(8, 128), :].T
            for j in range(8):
                for h in range(2):
                    ov[j, pl.ds(k + K * 8 * h, 8, stride=K), :] = t[16 * j + 8 * h : 16 * j + 8 * h + 8, :]
        return carry

    lax.fori_loop(0, K // 3, back, 0)
    outs = [pltpu.make_async_copy(ov.at[j, pl.ds(8, 512), :], o_h.at[:, pl.ds(128 * j, 128)], out_sem.at[j])
            for j in range(8)]
    for c in outs:
        c.start()
    for c in outs:
        c.wait()


def solution(mesh):
    rows, cols = mesh.shape["row"], mesh.shape["col"]

    def shards(elevation, ocean, outlet):
        scratch = [
            pltpu.VMEM((8, 512, 128), F32),
            pltpu.VMEM((8, 512, 128), jnp.int32),
            pltpu.VMEM((8, 512, 128), jnp.int32),
            pltpu.VMEM((2, 8, 528, 128), F32),
            pltpu.VMEM((2, 2, 8, 8, 128), F32),
            pltpu.VMEM((2, K, W, 128), F32),
            pltpu.VMEM((K + 2, W, 128), F32),
            pltpu.VMEM((K + 2, W, 128), F32),
            pltpu.VMEM((8, 528, 128), F32),
            pltpu.VMEM((3, 8, 32, 128), F32),
            pltpu.VMEM((3, 32, 128), F32),
            pltpu.VMEM((32, 128), F32),
            pltpu.VMEM((2, 3, 8, 128), F32),
            pltpu.VMEM((2, 48, 128), F32),
            pltpu.VMEM((128, 128), F32),
            pltpu.VMEM((4, 80, 128), F32),
            pltpu.VMEM((4, 16, 128), F32),
            pltpu.VMEM((K, 16, 128), F32),
            pltpu.VMEM((2, 2, 5, 8, 128), F32),
            pltpu.VMEM((2, 2, 5, 8, 128), F32),
            pltpu.VMEM((2, 2, 2, 8, 128), F32),
            pltpu.VMEM((2, 2, 2, 8, 128), F32),
            pltpu.VMEM((2, 128, 128), F32),
            pltpu.SemaphoreType.DMA((8, 3)),
            pltpu.SemaphoreType.DMA((8,)),
            pltpu.SemaphoreType.DMA((16,)),
            pltpu.SemaphoreType.DMA((16,)),
        ]
        return pl.pallas_call(
            lambda *refs: kernel(rows, cols, *refs),
            out_shape=jax.ShapeDtypeStruct((512, 1024), F32),
            in_specs=[pl.BlockSpec(memory_space=pl.ANY)] * 3,
            out_specs=pl.BlockSpec(memory_space=pl.ANY),
            scratch_shapes=scratch,
            name="fill",
            compiler_params=pltpu.CompilerParams(
                collective_id=0, has_side_effects=True, vmem_limit_bytes=48 << 20
            ),
        )(elevation, ocean, outlet)

    return jax.shard_map(
        shards,
        mesh=mesh,
        in_specs=(P("row", "col"), P("row", "col"), P("row", "col")),
        out_specs=P("row", "col"),
        check_vma=False,
    )
```

profile of v0, /device:TPU:0, one launch (start us, length us, event | category | flops | bytes accessed | tf_op | source)
XLA Modules:
  0.0 28.9 jit_solution(3069085483147505853)
XLA Ops:
  0.0 0.0 copy-start
  0.0 1.6 %copy-done = f32[512,1024]{1,0:T(8,128)S(1)} copy-done((f32[512,1024]{1,0:T(8,128)S(1)}, f32[512,1024]{1,0:T(8,128)}, u32[]{:S(2)}) %copy-start) | copy-done | bytes 2097176
  1.6 26.0 %fill.1 = f32[512,1024]{1,0:T(8,128)S(1)} custom-call(f32[512,1024]{1,0:T(8,128)S(1)} %copy-done, s32[512,1024]{1,0:T(8,128)} %refs_1_.1, s32[512,1024]{1,0:T(8,128)} %refs_2_.1), custom_call_target="tpu_custom_call" | custom-call | tf_op jit(solution)/shard_map/fill/pallas_call | solution.py:375
  27.6 1.3 %copy.5 = f32[512,1024]{1,0:T(8,128)} copy(f32[512,1024]{1,0:T(8,128)S(1)} %fill.1) | data formatting | bytes 4194304
Async XLA Ops:
  0.0 1.6 %copy-start = (f32[512,1024]{1,0:T(8,128)S(1)}, f32[512,1024]{1,0:T(8,128)}, u32[]{:S(2)}) copy-start(f32[512,1024]{1,0:T(8,128)} %refs_0_.1) | copy-start | bytes 6291460
where the time goes:
time: 29.1 us; the launch traced here: 28.9 us
  Pallas kernels  26 us (89%)
  local copies, waits for them, and re-layouts  2.91 us (10%)
    pallas_call x1, Pallas kernels, shards(): pl.pallas_call(lambda *refs: kernel(rows, cols, *refs), out_shape=jax.Sha...  26 us
    unnamed x3, local copies, waits for them, and re-layouts  2.91 us

commit v1 on v0

--- a/solution.py
+++ b/solution.py
@@ -105,45 +105,60 @@
     for dev in to:
         pl.semaphore_signal(barrier, inc=1, device_id=dev, device_id_type=MESH)
 
-    def loads(j):
-        at = pl.ds(128 * j, 128)
-        return [pltpu.make_async_copy(h.at[:, at], v.at[j], in_sem.at[j, i])
+    pieces = [((0, 16), (0, 8)), ((48, 16), (0, 8)), ((16, 32), (0, 1)), ((16, 32), (7, 1)), ((16, 16), (1, 6)), ((32, 16), (1, 6))]
+
+    def loads(p):
+        (r, nr), (j, nj) = pieces[p]
+        return [pltpu.make_async_copy(h.at[pl.ds(r, nr), pl.ds(j, nj)], v.at[pl.ds(r, nr), pl.ds(j, nj)], in_sem.at[p, i])
                 for i, (h, v) in enumerate(((e_h, ev), (oc_h, ocv), (ou_h, ouv)))]
 
-    for j in range(8):
-        for c in loads(j):
+    for p in range(6):
+        for c in loads(p):
             c.start()
 
-    for j in range(8):
-        for c in loads(j):
+    def arrived(p):
+        for c in loads(p):
             c.wait()
 
-        def group(grp, carry, j=j):
-            gmin, lmin, gmax = [], [], []
-            for c in range(8):
-                gs, ls = [], []
-                for h in range(2):
-                    r = pl.multiple_of(grp * 128 + 16 * c + 8 * h, 8)
-                    oc = ocv[j, pl.ds(r, 8), :] == 1
-                    ou = ouv[j, pl.ds(r, 8), :] == 1
-                    g = jnp.where(oc, F32(0.0), ev[j, pl.ds(r, 8), :])
-                    lk = jnp.where(oc | ou, g, F32(HUGE))
-                    gl[0, j, pl.ds(r + 8, 8), :] = g
-                    gl[1, j, pl.ds(r + 8, 8), :] = lk
-                    gs.append(g)
-                    ls.append(lk)
-                gmin.append(jnp.minimum(*gs))
-                lmin.append(jnp.minimum(*ls))
-                gmax.append(jnp.maximum(*gs))
-            at = pl.ds(pl.multiple_of(grp * 8, 8), 8)
-            ca[0, j, at, :] = tree(gmin, (4, 2, 1), 0, sub, jnp.minimum)
-            ca[1, j, at, :] = tree(lmin, (4, 2, 1), 0, sub, jnp.minimum)
-            ca[2, j, at, :] = tree(gmax, (4, 2, 1), 0, sub, jnp.maximum)
+    def group(grp, j):
+        gmin, lmin, gmax = [], [], []
+        for c in range(8):
+            gs, ls = [], []
+            for h in range(2):
+                r = grp * 16 + 2 * c + h
+                oc = ocv[r, j] == 1
+                ou = ouv[r, j] == 1
+                g = jnp.where(oc, F32(0.0), ev[r, j])
+                lk = jnp.where(oc | ou, g, F32(HUGE))
+                at = pl.ds(8 * r + 8, 8)
+                gl[0, j, at, :] = g
+                gl[1, j, at, :] = lk
+                gs.append(g)
+                ls.append(lk)
+            gmin.append(jnp.minimum(*gs))
+            lmin.append(jnp.minimum(*ls))
+            gmax.append(jnp.maximum(*gs))
+        at = pl.ds(grp * 8, 8)
+        ca[0, j, at, :] = tree(gmin, (4, 2, 1), 0, sub, jnp.minimum)
+        ca[1, j, at, :] = tree(lmin, (4, 2, 1), 0, sub, jnp.minimum)
+        ca[2, j, at, :] = tree(gmax, (4, 2, 1), 0, sub, jnp.maximum)
+
+    def groups(grp, lo, hi):
+        def body(j, carry):
+            group(grp, j)
             return carry
 
-        lax.fori_loop(0, 4, group, 0)
-
-    pl.semaphore_wait(barrier, 8)
+        lax.fori_loop(lo, hi, body, 0, unroll=2)
+
+    arrived(0)
+    groups(0, 0, 8)
+    arrived(1)
+    groups(3, 0, 8)
+    for j, p in ((0, 2), (7, 3)):
+        arrived(p)
+        group(1, j)
+        group(2, j)
+
 
     def copy(i, src, dst, d):
         return pltpu.make_async_remote_copy(src_ref=src, dst_ref=dst, send_sem=send.at[i], recv_sem=recv.at[i],
@@ -152,21 +167,30 @@
     copies = [None] * 16
     copies[N_] = copy(N_, gl.at[:, :, pl.ds(8, 8), :], halo.at[1], N_)
     copies[S_] = copy(S_, gl.at[:, :, pl.ds(512, 8), :], halo.at[0], S_)
-    copies[N_].start()
-    copies[S_].start()
 
     index = jnp.where((lane >= 8) & (lane < 72), 16 * ((lane - 8) & 7) + 2 * ((lane - 8) >> 3), 0)
-    for a in range(3):
-        op = jnp.maximum if a == 2 else jnp.minimum
-        for grp in range(4):
-            x = tree([ca[a, j, pl.ds(8 * grp, 8), :] for j in range(8)], (8, 4, 2), 1, lane, op)
+
+    def cells(grp, js):
+        out = []
+        for a in range(3):
+            op = jnp.maximum if a == 2 else jnp.minimum
+            x = tree([ca[a, j, pl.ds(8 * grp, 8), :] for j in js], (8, 4, 2), 1, lane, op)
             x = op(x, pltpu.roll(x, 127, 1))
-            cp[a, pl.ds(8 * grp, 8), :] = jnp.take_along_axis(x, index, axis=1)
+            out.append(jnp.take_along_axis(x, index, axis=1))
+        return out
+
+    def keep(grp, x):
+        for a in range(3):
+            cp[a, pl.ds(8 * grp, 8), :] = x[a]
+
     for grp in range(4):
-        at = pl.ds(8 * grp, 8)
-        pk[at, :] = jnp.where(((lane >= 8) & (lane < 16)) | ((lane >= 64) & (lane < 72)), cp[0, at, :],
-                              jnp.where(((lane >= 16) & (lane < 24)) | ((lane >= 72) & (lane < 80)),
-                                        pltpu.roll(cp[1, at, :], 8, 1), pltpu.roll(cp[2, at, :], 16, 1)))
+        x = cells(grp, range(8) if grp in (0, 3) else (0, 0, 0, 0, 7, 7, 7, 7))
+        if grp in (0, 3):
+            keep(grp, x)
+        pk[pl.ds(8 * grp, 8), :] = jnp.where(
+            ((lane >= 8) & (lane < 16)) | ((lane >= 64) & (lane < 72)), x[0],
+            jnp.where(((lane >= 16) & (lane < 24)) | ((lane >= 72) & (lane < 80)),
+                      pltpu.roll(x[1], 8, 1), pltpu.roll(x[2], 16, 1)))
     top, bottom = pl.ds(0, 8), pl.ds(24, 8)
     copies[8 + N_] = copy(8 + N_, cp.at[:, top, :], cn.at[1], N_)
     copies[8 + S_] = copy(8 + S_, cp.at[:, bottom, :], cn.at[0], S_)
@@ -176,8 +200,6 @@
     copies[8 + NE_] = copy(8 + NE_, pk.at[top, :], pwe.at[0, pl.ds(40, 8), :], NE_)
     copies[8 + SW_] = copy(8 + SW_, pk.at[bottom, :], pwe.at[1, pl.ds(0, 8), :], SW_)
     copies[8 + SE_] = copy(8 + SE_, pk.at[bottom, :], pwe.at[0, pl.ds(0, 8), :], SE_)
-    for i in (NW_, NE_, SW_, SE_, W_, E_, N_, S_):
-        copies[8 + i].start()
 
     for arr in range(2):
         for grp in range(5):
@@ -200,8 +222,16 @@
     copies[NE_] = copy(NE_, cs.at[1, 0], cr.at[0, 1], NE_)
     copies[SW_] = copy(SW_, cs.at[0, 1], cr.at[1, 0], SW_)
     copies[SE_] = copy(SE_, cs.at[1, 1], cr.at[0, 0], SE_)
-    for i in (NW_, NE_, SW_, SE_, W_, E_):
+    pl.semaphore_wait(barrier, 8)
+    for i in (W_, E_, NW_, NE_, SW_, SE_, N_, S_):
         copies[i].start()
+        copies[8 + i].start()
+
+    for grp in (1, 2):
+        arrived(3 + grp)
+        groups(grp, 1, 7)
+    for grp in (1, 2):
+        keep(grp, cells(grp, range(8)))
 
     def turn(i, carry):
         for u in range(3):
@@ -213,23 +243,30 @@
 
     lax.fori_loop(0, K // 3, turn, 0)
 
-    for i in range(8):
+    for arr in range(2):
+        for k in range(8, 25):
+            tt[arr, k, pl.ds(0, 8), :] = pltpu.roll(tt[arr, k, pl.ds(128, 8), :], 16, 1)
+            tt[arr, k, pl.ds(136, 8), :] = pltpu.roll(tt[arr, k, pl.ds(8, 8), :], 112, 1)
+
+    for i in range(16):
         copies[i].wait()
     strip = lane & 15
     for arr in range(2):
-        parts = []
-        for j in range(8):
-            parts.append(jnp.where(north, F32(HUGE), halo[0, arr, j, :, :]))
-            parts.append(jnp.where(south, F32(HUGE), halo[1, arr, j, :, :]))
-        ht[arr, :, :] = jnp.concatenate(parts, axis=0).T
+        up = [jnp.where(north, F32(HUGE), halo[0, arr, j, :, :]) for j in range(8)]
+        down = [pltpu.roll(jnp.where(south, F32(HUGE), halo[1, arr, j, :, :]), 7, 0) for j in range(8)]
+        for odd in range(2):
+            parts = []
+            for j in range(8):
+                parts.append(jnp.where((sub & 1) == odd, up[j], down[(j + 7) % 8]))
+                parts.append(down[j])
+            ht[arr, odd, :, :] = jnp.concatenate(parts, axis=0).T
     for arr in range(2):
         for k in range(8):
             for i in range(16):
                 at = pl.ds(8 + 8 * i, 8)
-                h = ht[arr, pl.ds(8 * i, 8), :]
-                tt[arr, k, at, :] = jnp.where(strip == 0, pltpu.roll(h, (128 - k) % 128, 1), tt[arr, k, at, :])
-                kk = k + 25
-                tt[arr, kk, at, :] = jnp.where(strip == 15, pltpu.roll(h, 32 - kk, 1), tt[arr, kk, at, :])
+                h = pltpu.roll(ht[arr, k % 2, pl.ds(8 * i, 8), :], (128 - k) % 128, 1)
+                tt[arr, k, at, :] = jnp.where(strip == 0, h, tt[arr, k, at, :])
+                tt[arr, k + 25, at, :] = jnp.where(strip == 15, h, tt[arr, k + 25, at, :])
         edge = []
         for side in range(2):
             up = jnp.where(north, F32(HUGE), cr[side, 0, arr, :, :])
@@ -241,15 +278,14 @@
             edge.append(e)
         for k in range(K):
             i = k % 8
-            own = pltpu.roll(tt[arr, k, pl.ds(128, 8), :], 16, 1)
+            inner = 8 <= k < 25
+            own = tt[arr, k, pl.ds(0, 8), :] if inner else pltpu.roll(tt[arr, k, pl.ds(128, 8), :], 16, 1)
             got = pltpu.roll(edge[0][k // 8], (128 - 16 * i) % 128, 1)
             tt[arr, k, pl.ds(0, 8), :] = jnp.where(lane < 16, got, own)
-            own = pltpu.roll(tt[arr, k, pl.ds(8, 8), :], 112, 1)
+            own = tt[arr, k, pl.ds(136, 8), :] if inner else pltpu.roll(tt[arr, k, pl.ds(8, 8), :], 112, 1)
             got = pltpu.roll(edge[1][k // 8], (112 - 16 * i) % 128, 1)
             tt[arr, k, pl.ds(136, 8), :] = jnp.where(lane >= 112, got, own)
 
-    for i in range(8):
-        copies[8 + i].wait()
     ext = []
     for a in range(3):
         tiles = []
@@ -322,15 +358,15 @@
     lax.fori_loop(0, 4, two, 0)
 
     def back(i, carry):
-        for u in range(3):
-            k = 3 * i + u
+        for u in range(11):
+            k = 11 * i + u
             t = va[k + 1, pl.ds(8, 128), :].T
             for j in range(8):
                 for h in range(2):
                     ov[j, pl.ds(k + K * 8 * h, 8, stride=K), :] = t[16 * j + 8 * h : 16 * j + 8 * h + 8, :]
         return carry
 
-    lax.fori_loop(0, K // 3, back, 0)
+    lax.fori_loop(0, K // 11, back, 0)
     outs = [pltpu.make_async_copy(ov.at[j, pl.ds(8, 512), :], o_h.at[:, pl.ds(128 * j, 128)], out_sem.at[j])
             for j in range(8)]
     for c in outs:
@@ -339,14 +375,18 @@
         c.wait()
 
 
+def tiled(x):
+    return x.reshape(64, 8, 8, 128).transpose(0, 2, 1, 3)
+
+
 def solution(mesh):
     rows, cols = mesh.shape["row"], mesh.shape["col"]
 
     def shards(elevation, ocean, outlet):
         scratch = [
-            pltpu.VMEM((8, 512, 128), F32),
-            pltpu.VMEM((8, 512, 128), jnp.int32),
-            pltpu.VMEM((8, 512, 128), jnp.int32),
+            pltpu.VMEM((64, 8, 8, 128), F32),
+            pltpu.VMEM((64, 8, 8, 128), jnp.int32),
+            pltpu.VMEM((64, 8, 8, 128), jnp.int32),
             pltpu.VMEM((2, 8, 528, 128), F32),
             pltpu.VMEM((2, 2, 8, 8, 128), F32),
             pltpu.VMEM((2, K, W, 128), F32),
@@ -366,8 +406,8 @@
             pltpu.VMEM((2, 2, 5, 8, 128), F32),
             pltpu.VMEM((2, 2, 2, 8, 128), F32),
             pltpu.VMEM((2, 2, 2, 8, 128), F32),
-            pltpu.VMEM((2, 128, 128), F32),
-            pltpu.SemaphoreType.DMA((8, 3)),
+            pltpu.VMEM((2, 2, 128, 128), F32),
+            pltpu.SemaphoreType.DMA((6, 3)),
             pltpu.SemaphoreType.DMA((8,)),
             pltpu.SemaphoreType.DMA((16,)),
             pltpu.SemaphoreType.DMA((16,)),
@@ -380,9 +420,9 @@
             scratch_shapes=scratch,
             name="fill",
             compiler_params=pltpu.CompilerParams(
-                collective_id=0, has_side_effects=True, vmem_limit_bytes=48 << 20
+                collective_id=0, has_side_effects=True, vmem_limit_bytes=50 << 20
             ),
-        )(elevation, ocean, outlet)
+        )(tiled(elevation), tiled(ocean), tiled(outlet))
 
     return jax.shard_map(
         shards,

time: 29.1 us -> 24.4 us (0.84)
  Pallas kernels: 26 us -> 22.9 us
  local copies, waits for them, and re-layouts: 2.91 us -> 1.32 us
    pallas_call x1, Pallas kernels: 26 us -> 22.9 us  [shards(): pl.pallas_call(lambda *refs: kernel(rows, cols, *refs), out_shape=jax.Sha...]
    unnamed x3 -> x1, local copies, waits for them, and re-layouts: 2.91 us -> 1.32 us
where the time goes in v1:
time: 24.4 us; the launch traced here: 24.3 us
  Pallas kernels  22.9 us (94%)
  local copies, waits for them, and re-layouts  1.32 us (5%)
    pallas_call x1, Pallas kernels, shards(): pl.pallas_call(lambda *refs: kernel(rows, cols, *refs), out_shape=jax.Sha...  22.9 us
    unnamed x1, local copies, waits for them, and re-layouts  1.32 us

profile of v1, /device:TPU:0, one launch (start us, length us, event | category | flops | bytes accessed | tf_op | source)
XLA Modules:
  0.0 24.3 jit_solution(12306426699613836112)
XLA Ops:
  0.0 22.9 %fill.1 = f32[512,1024]{1,0:T(8,128)S(1)} custom-call(f32[64,8,8,128]{3,2,1,0:T(8,128)} %bitcast.9, s32[64,8,8,128]{3,2,1,0:T(8,128)} %bitcast.10, s32[64,8,8,128]{3,2,1,0:T(8,128)} %bitcast.11), custom_call_target="tpu_custom_call" | custom-call | tf_op jit(solution)/shard_map/fill/pallas_call | solution.py:415
  22.9 1.3 %copy.5 = f32[512,1024]{1,0:T(8,128)} copy(f32[512,1024]{1,0:T(8,128)S(1)} %fill.1) | data formatting | bytes 4194304

commit v2 on v1

--- a/solution.py
+++ b/solution.py
@@ -90,11 +90,11 @@
         pair(2 + 2 * i)
         return c
 
-    lax.fori_loop(0, (K - 3) // 2, body, 0)
-
-
-def kernel(rows, cols, e_h, oc_h, ou_h, o_h, ev, ocv, ouv, gl, halo, tt, va, vb, ov, ca, cp, pk, cn, pwe, cf, zz,
-           yy, xb, fs, fr, cs, cr, ht, in_sem, out_sem, send, recv):
+    lax.fori_loop(0, (K - 3) // 2, body, 0, unroll=3)
+
+
+def kernel(rows, cols, e_h, oc_h, ou_h, o_h, ev, ocv, ouv, gl, tt, va, vb, ov, ca, cp, cf, zz,
+           yy, xb, rs, rr, es, er, ds, dr, ht, in_sem, out_sem, send, recv):
     lane = lanes()
     sub = subs()
     north = lax.axis_index("row") == 0
@@ -102,8 +102,8 @@
     to = [neighbour(d, rows, cols) for d in DIRS]
 
     barrier = pltpu.get_barrier_semaphore()
-    for dev in to:
-        pl.semaphore_signal(barrier, inc=1, device_id=dev, device_id_type=MESH)
+    for i in (NW_, NE_, SW_, SE_, W_, E_, N_, S_):
+        pl.semaphore_signal(barrier, inc=1, device_id=to[i], device_id_type=MESH)
 
     pieces = [((0, 16), (0, 8)), ((48, 16), (0, 8)), ((16, 32), (0, 1)), ((16, 32), (7, 1)), ((16, 16), (1, 6)), ((32, 16), (1, 6))]
 
@@ -160,13 +160,18 @@
         group(2, j)
 
 
-    def copy(i, src, dst, d):
-        return pltpu.make_async_remote_copy(src_ref=src, dst_ref=dst, send_sem=send.at[i], recv_sem=recv.at[i],
+    def copy(d, src, dst):
+        return pltpu.make_async_remote_copy(src_ref=src, dst_ref=dst, send_sem=send.at[d], recv_sem=recv.at[d],
                                             device_id=to[d], device_id_type=MESH)
 
-    copies = [None] * 16
-    copies[N_] = copy(N_, gl.at[:, :, pl.ds(8, 8), :], halo.at[1], N_)
-    copies[S_] = copy(S_, gl.at[:, :, pl.ds(512, 8), :], halo.at[0], S_)
+    copies = [copy(N_, rs.at[0], rr.at[1]), copy(S_, rs.at[1], rr.at[0]),
+              copy(W_, es.at[0], er.at[1]), copy(E_, es.at[1], er.at[0]),
+              copy(NW_, ds.at[0, 0], dr.at[1, 1]), copy(NE_, ds.at[1, 0], dr.at[0, 1]),
+              copy(SW_, ds.at[0, 1], dr.at[1, 0]), copy(SE_, ds.at[1, 1], dr.at[0, 0])]
+    for arr in range(2):
+        for j in range(8):
+            rs[0, 8 * arr + j] = gl[arr, j, pl.ds(8, 8), :]
+            rs[1, 8 * arr + j] = gl[arr, j, pl.ds(512, 8), :]
 
     index = jnp.where((lane >= 8) & (lane < 72), 16 * ((lane - 8) & 7) + 2 * ((lane - 8) >> 3), 0)
 
@@ -183,24 +188,22 @@
         for a in range(3):
             cp[a, pl.ds(8 * grp, 8), :] = x[a]
 
+    packs = []
     for grp in range(4):
         x = cells(grp, range(8) if grp in (0, 3) else (0, 0, 0, 0, 7, 7, 7, 7))
         if grp in (0, 3):
             keep(grp, x)
-        pk[pl.ds(8 * grp, 8), :] = jnp.where(
+            for a in range(3):
+                rs[grp // 3, 16 + a] = x[a]
+        pk = jnp.where(
             ((lane >= 8) & (lane < 16)) | ((lane >= 64) & (lane < 72)), x[0],
             jnp.where(((lane >= 16) & (lane < 24)) | ((lane >= 72) & (lane < 80)),
                       pltpu.roll(x[1], 8, 1), pltpu.roll(x[2], 16, 1)))
-    top, bottom = pl.ds(0, 8), pl.ds(24, 8)
-    copies[8 + N_] = copy(8 + N_, cp.at[:, top, :], cn.at[1], N_)
-    copies[8 + S_] = copy(8 + S_, cp.at[:, bottom, :], cn.at[0], S_)
-    copies[8 + W_] = copy(8 + W_, pk, pwe.at[1, pl.ds(8, 32), :], W_)
-    copies[8 + E_] = copy(8 + E_, pk, pwe.at[0, pl.ds(8, 32), :], E_)
-    copies[8 + NW_] = copy(8 + NW_, pk.at[top, :], pwe.at[1, pl.ds(40, 8), :], NW_)
-    copies[8 + NE_] = copy(8 + NE_, pk.at[top, :], pwe.at[0, pl.ds(40, 8), :], NE_)
-    copies[8 + SW_] = copy(8 + SW_, pk.at[bottom, :], pwe.at[1, pl.ds(0, 8), :], SW_)
-    copies[8 + SE_] = copy(8 + SE_, pk.at[bottom, :], pwe.at[0, pl.ds(0, 8), :], SE_)
-
+        packs.append(pk)
+        for side in range(2):
+            if grp in (0, 3):
+                ds[side, grp // 3, 1] = pk
+    ends = [[None] * 5, [None] * 5]
     for arr in range(2):
         for grp in range(5):
             parts = []
@@ -210,22 +213,24 @@
                     at = pl.ds(k + K * s, 8, stride=K)
                     parts.append(jnp.where(lane < 64, gl[arr, 0, at, :], gl[arr, 7, at, :]))
             t = jnp.concatenate(parts, axis=0).T
-            fs[0, arr, grp, :, :] = t[0:8, :]
-            fs[1, arr, grp, :, :] = t[120:128, :]
-        for side in range(2):
-            cs[side, 0, arr, :, :] = pltpu.roll(fs[side, arr, 1, :, :], 31, 1)
-            cs[side, 1, arr, :, :] = pltpu.roll(
-                jnp.where(lane == 15, fs[side, arr, 3, :, :], fs[side, arr, 2, :, :]), 97, 1)
-    copies[W_] = copy(W_, fs.at[0], fr.at[1], W_)
-    copies[E_] = copy(E_, fs.at[1], fr.at[0], E_)
-    copies[NW_] = copy(NW_, cs.at[0, 0], cr.at[1, 1], NW_)
-    copies[NE_] = copy(NE_, cs.at[1, 0], cr.at[0, 1], NE_)
-    copies[SW_] = copy(SW_, cs.at[0, 1], cr.at[1, 0], SW_)
-    copies[SE_] = copy(SE_, cs.at[1, 1], cr.at[0, 0], SE_)
+            ends[arr][grp] = (t[0:8, :], t[120:128, :])
+            for side in range(2):
+                if grp < 4:
+                    es[side, 4 * arr + grp] = ends[arr][grp][side]
+    strip = lane & 15
+    for side in range(2):
+        x = jnp.where(lane < 16, ends[0][4][side], pltpu.roll(ends[1][4][side], 16, 1))
+        for t in range(4):
+            y = pltpu.roll(packs[t], (24 * t + (24 if side == 0 else 96)) % 128, 1)
+            x = jnp.where(lane < 32 + 24 * t, x, y)
+        es[side, 8] = x
+        g, lk = (pltpu.roll(ends[arr][1][side], 31 + arr, 1) for arr in range(2))
+        ds[side, 0, 0] = jnp.where(strip == 15, g, lk)
+        g, lk = (pltpu.roll(jnp.where(lane == 15, ends[arr][3][side], ends[arr][2][side]), 97 + arr, 1) for arr in range(2))
+        ds[side, 1, 0] = jnp.where(strip == 0, g, lk)
     pl.semaphore_wait(barrier, 8)
     for i in (W_, E_, NW_, NE_, SW_, SE_, N_, S_):
         copies[i].start()
-        copies[8 + i].start()
 
     for grp in (1, 2):
         arrived(3 + grp)
@@ -248,12 +253,11 @@
             tt[arr, k, pl.ds(0, 8), :] = pltpu.roll(tt[arr, k, pl.ds(128, 8), :], 16, 1)
             tt[arr, k, pl.ds(136, 8), :] = pltpu.roll(tt[arr, k, pl.ds(8, 8), :], 112, 1)
 
-    for i in range(16):
+    for i in range(8):
         copies[i].wait()
-    strip = lane & 15
     for arr in range(2):
-        up = [jnp.where(north, F32(HUGE), halo[0, arr, j, :, :]) for j in range(8)]
-        down = [pltpu.roll(jnp.where(south, F32(HUGE), halo[1, arr, j, :, :]), 7, 0) for j in range(8)]
+        up = [jnp.where(north, F32(HUGE), rr[0, 8 * arr + j]) for j in range(8)]
+        down = [pltpu.roll(jnp.where(south, F32(HUGE), rr[1, 8 * arr + j]), 7, 0) for j in range(8)]
         for odd in range(2):
             parts = []
             for j in range(8):
@@ -269,9 +273,11 @@
                 tt[arr, k + 25, at, :] = jnp.where(strip == 15, h, tt[arr, k + 25, at, :])
         edge = []
         for side in range(2):
-            up = jnp.where(north, F32(HUGE), cr[side, 0, arr, :, :])
-            down = jnp.where(south, F32(HUGE), cr[side, 1, arr, :, :])
-            e = [fr[side, arr, grp, :, :] for grp in range(5)]
+            corner = [pltpu.roll(dr[side, i, 0], 127, 1) if arr else dr[side, i, 0] for i in range(2)]
+            up = jnp.where(north, F32(HUGE), corner[0])
+            down = jnp.where(south, F32(HUGE), corner[1])
+            e = [er[side, 4 * arr + grp] for grp in range(4)]
+            e.append(pltpu.roll(er[side, 8], 112, 1) if arr else er[side, 8])
             e[0] = jnp.where(strip == 0, up, e[0])
             e[3] = jnp.where((strip == 15) & (lane >= 31), down, e[3])
             e[4] = jnp.where(lane == 15, down, e[4])
@@ -286,13 +292,19 @@
             got = pltpu.roll(edge[1][k // 8], (112 - 16 * i) % 128, 1)
             tt[arr, k, pl.ds(136, 8), :] = jnp.where(lane >= 112, got, own)
 
+    rings = []
+    for t in range(6):
+        if t in (0, 5):
+            west, east = (dr[i, t // 5, 1] for i in range(2))
+        else:
+            west, east = (pltpu.roll(er[i, 8], (b - 24 * t + 24) % 128, 1) for i, b in ((0, 32), (1, 104)))
+        rings.append(jnp.where(lane < 64, east, west))
     ext = []
     for a in range(3):
         tiles = []
         for t in range(6):
-            at = pl.ds(8 * t, 8)
-            ring = pltpu.roll(jnp.where(lane < 64, pwe[1, at, :], pwe[0, at, :]), 64 - 8 * a, 1)
-            mid = cn[0, a, :, :] if t == 0 else cn[1, a, :, :] if t == 5 else cp[a, pl.ds(8 * t - 8, 8), :]
+            ring = pltpu.roll(rings[t], 64 - 8 * a, 1)
+            mid = rr[0, 16 + a] if t == 0 else rr[1, 16 + a] if t == 5 else cp[a, pl.ds(8 * t - 8, 8), :]
             x = jnp.where((lane >= 8) & (lane < 72), mid, ring)
             if t == 0:
                 x = jnp.where(north, F32(HUGE), x)
@@ -388,29 +400,27 @@
             pltpu.VMEM((64, 8, 8, 128), jnp.int32),
             pltpu.VMEM((64, 8, 8, 128), jnp.int32),
             pltpu.VMEM((2, 8, 528, 128), F32),
-            pltpu.VMEM((2, 2, 8, 8, 128), F32),
             pltpu.VMEM((2, K, W, 128), F32),
             pltpu.VMEM((K + 2, W, 128), F32),
             pltpu.VMEM((K + 2, W, 128), F32),
             pltpu.VMEM((8, 528, 128), F32),
             pltpu.VMEM((3, 8, 32, 128), F32),
             pltpu.VMEM((3, 32, 128), F32),
-            pltpu.VMEM((32, 128), F32),
-            pltpu.VMEM((2, 3, 8, 128), F32),
-            pltpu.VMEM((2, 48, 128), F32),
             pltpu.VMEM((128, 128), F32),
             pltpu.VMEM((4, 80, 128), F32),
             pltpu.VMEM((4, 16, 128), F32),
             pltpu.VMEM((K, 16, 128), F32),
-            pltpu.VMEM((2, 2, 5, 8, 128), F32),
-            pltpu.VMEM((2, 2, 5, 8, 128), F32),
+            pltpu.VMEM((2, 19, 8, 128), F32),
+            pltpu.VMEM((2, 19, 8, 128), F32),
+            pltpu.VMEM((2, 9, 8, 128), F32),
+            pltpu.VMEM((2, 9, 8, 128), F32),
             pltpu.VMEM((2, 2, 2, 8, 128), F32),
             pltpu.VMEM((2, 2, 2, 8, 128), F32),
             pltpu.VMEM((2, 2, 128, 128), F32),
             pltpu.SemaphoreType.DMA((6, 3)),
             pltpu.SemaphoreType.DMA((8,)),
-            pltpu.SemaphoreType.DMA((16,)),
-            pltpu.SemaphoreType.DMA((16,)),
+            pltpu.SemaphoreType.DMA((8,)),
+            pltpu.SemaphoreType.DMA((8,)),
         ]
         return pl.pallas_call(
             lambda *refs: kernel(rows, cols, *refs),

time: 24.4 us -> 23.3 us (0.955)
  Pallas kernels: 22.9 us -> 21.8 us
    pallas_call x1, Pallas kernels: 22.9 us -> 21.8 us  [shards(): pl.pallas_call(lambda *refs: kernel(rows, cols, *refs), out_shape=jax.Sha...]
where the time goes in v2:
time: 23.3 us; the launch traced here: 23.2 us
  Pallas kernels  21.8 us (94%)
  local copies, waits for them, and re-layouts  1.32 us (6%)
    pallas_call x1, Pallas kernels, shards(): pl.pallas_call(lambda *refs: kernel(rows, cols, *refs), out_shape=jax.Sha...  21.8 us
    unnamed x1, local copies, waits for them, and re-layouts  1.32 us

profile of v2, /device:TPU:0, one launch (start us, length us, event | category | flops | bytes accessed | tf_op | source)
XLA Modules:
  0.0 23.2 jit_solution(4146507292408806049)
XLA Ops:
  0.0 21.8 %fill.1 = f32[512,1024]{1,0:T(8,128)S(1)} custom-call(f32[64,8,8,128]{3,2,1,0:T(8,128)} %bitcast.9, s32[64,8,8,128]{3,2,1,0:T(8,128)} %bitcast.10, s32[64,8,8,128]{3,2,1,0:T(8,128)} %bitcast.11), custom_call_target="tpu_custom_call" | custom-call | tf_op jit(solution)/shard_map/fill/pallas_call | solution.py:425
  21.8 1.3 %copy.5 = f32[512,1024]{1,0:T(8,128)} copy(f32[512,1024]{1,0:T(8,128)S(1)} %fill.1) | data formatting | bytes 4194304

commit v3 on v2

v3 whole, which is shorter than its diff:
```python
import jax
import jax.numpy as jnp
from jax import lax
from jax.experimental import pallas as pl
from jax.experimental.pallas import tpu as pltpu
from jax.sharding import PartitionSpec as P

MESH = pl.DeviceIdType.MESH
HUGE = 1e30
FINE_STEP = 2.0 ** (-10)
COARSE_STEP = 2.0 ** (-6)
F32 = jnp.float32

KI, KE, KS = 25, 11, 6
AJ, AS = 18, 11

DIRS = [(-1, 0), (1, 0), (0, -1), (0, 1), (-1, -1), (-1, 1), (1, -1), (1, 1)]
N_, S_, W_, E_, NW_, NE_, SW_, SE_ = range(8)
OPP = [S_, N_, E_, W_, SE_, SW_, NE_, NW_]


def lanes():
    return lax.broadcasted_iota(jnp.int32, (8, 128), 1)


def subs():
    return lax.broadcasted_iota(jnp.int32, (8, 128), 0)


def merge(a, b, w, axis, pos, op):
    size = 8 if axis == 0 else 128
    low = (pos & w) == 0
    p = jnp.where(low, a, b)
    q = jnp.where(low, pltpu.roll(a, size - w, axis), pltpu.roll(b, w, axis))
    return op(p, q)


def tree(xs, ws, axis, pos, op):
    for w in ws:
        half = len(xs) // 2
        xs = [merge(xs[i], xs[i + half], w, axis, pos, op) for i in range(half)]
    return xs[0]


def neighbour(d, rows, cols):
    r = lax.axis_index("row")
    c = lax.axis_index("col")
    return (lax.rem(r + d[0] + rows, rows), lax.rem(c + d[1] + cols, cols))


def sweep(src, dst, g, K, A, loop):
    def row(ref, k):
        return [ref[k, pl.ds(a, 8, stride=A), :] for a in range(A)]

    def across(vm):
        before = pltpu.roll(vm[A - 1], 1, 0)
        after = pltpu.roll(vm[0], 7, 0)
        m = [None] * A
        for a in range(0, A - 1, 2):
            q = jnp.minimum(vm[a], vm[a + 1])
            m[a] = jnp.minimum(vm[a - 1] if a else before, q)
            m[a + 1] = jnp.minimum(q, vm[a + 2] if a + 2 < A else after)
        if A % 2:
            m[A - 1] = jnp.minimum(jnp.minimum(vm[A - 2], vm[A - 1]), after)
        return m

    def put(k, v, m):
        out = []
        for a in range(A):
            x = jnp.maximum(g[k, pl.ds(a, 8, stride=A), :], jnp.minimum(v[a], m[a] + FINE_STEP))
            dst[k + 1, pl.ds(a, 8, stride=A), :] = x
            out.append(x)
        return out

    def pair(k):
        v0, v1, v2, v3 = (row(src, k + i) for i in range(4))
        p = [jnp.minimum(x, y) for x, y in zip(v1, v2)]
        m0 = across([jnp.minimum(x, y) for x, y in zip(v0, p)])
        m1 = across([jnp.minimum(x, y) for x, y in zip(p, v3)])
        return put(k, v1, m0), put(k + 1, v2, m1)

    if K % 2:
        v0, v1, v2 = (row(src, K - 1 + i) for i in range(3))
        last = put(K - 1, v1, across([jnp.minimum(jnp.minimum(x, y), z) for x, y, z in zip(v0, v1, v2)]))
    else:
        last = pair(K - 2)[1]
    for a in range(A):
        dst[0, pl.ds(a, 8, stride=A), :] = pltpu.roll(last[a], 1, 1)
    first, _ = pair(0)
    for a in range(A):
        dst[K + 1, pl.ds(a, 8, stride=A), :] = pltpu.roll(first[a], 127, 1)

    count = (K - 3) // 2 if K % 2 else (K - 4) // 2
    if loop:
        def body(i, c):
            pair(2 + 2 * i)
            return c

        lax.fori_loop(0, count, body, 0)
    else:
        for i in range(count):
            pair(2 + 2 * i)


def kernel(rows, cols, e_h, oc_h, ou_h, o_h, ev, ocv, ouv, gl, ti, te, ts, vi, wi, ve, we, vs, ws, ov, oe, ca, cp, cf, zz,
           yy, xb, cb, rs, rr, es, er, ds, dr, ht, in_sem, out_sem, send, recv):
    lane = lanes()
    sub = subs()
    north = lax.axis_index("row") == 0
    south = lax.axis_index("row") == rows - 1
    to = [neighbour(d, rows, cols) for d in DIRS]

    barrier = pltpu.get_barrier_semaphore()
    for i in (NW_, NE_, SW_, SE_, W_, E_, N_, S_):
        pl.semaphore_signal(barrier, inc=1, device_id=to[i], device_id_type=MESH)

    pieces = [((0, 16), (0, 8)), ((48, 16), (0, 8)), ((16, 32), (0, 1)), ((16, 32), (7, 1)), ((16, 16), (1, 6)), ((32, 16), (1, 6))]

    def loads(p):
        (r, nr), (j, nj) = pieces[p]
        return [pltpu.make_async_copy(h.at[pl.ds(r, nr), pl.ds(j, nj)], v.at[pl.ds(r, nr), pl.ds(j, nj)], in_sem.at[p, i])
                for i, (h, v) in enumerate(((e_h, ev), (oc_h, ocv), (ou_h, ouv)))]

    for p in range(6):
        for c in loads(p):
            c.start()

    def arrived(p):
        for c in loads(p):
            c.wait()

    def group(grp, j):
        gmin, lmin, gmax = [], [], []
        for c in range(8):
            gs, ls = [], []
            for h in range(2):
                r = grp * 16 + 2 * c + h
                oc = ocv[r, j] == 1
                ou = ouv[r, j] == 1
                g = jnp.where(oc, F32(0.0), ev[r, j])
                lk = jnp.where(oc | ou, g, F32(HUGE))
                at = pl.ds(8 * r + 8, 8)
                gl[0, j, at, :] = g
                gl[1, j, at, :] = lk
                gs.append(g)
                ls.append(lk)
            gmin.append(jnp.minimum(*gs))
            lmin.append(jnp.minimum(*ls))
            gmax.append(jnp.maximum(*gs))
        at = pl.ds(grp * 8, 8)
        ca[0, j, at, :] = tree(gmin, (4, 2, 1), 0, sub, jnp.minimum)
        ca[1, j, at, :] = tree(lmin, (4, 2, 1), 0, sub, jnp.minimum)
        ca[2, j, at, :] = tree(gmax, (4, 2, 1), 0, sub, jnp.maximum)

    def groups(grp, lo, hi):
        def body(j, carry):
            group(grp, j)
            return carry

        lax.fori_loop(lo, hi, body, 0, unroll=2)

    arrived(0)
    groups(0, 0, 8)
    arrived(1)
    groups(3, 0, 8)
    for j, p in ((0, 2), (7, 3)):
        arrived(p)
        group(1, j)
        group(2, j)


    def copy(d, src, dst):
        return pltpu.make_async_remote_copy(src_ref=src, dst_ref=dst, send_sem=send.at[d], recv_sem=recv.at[d],
                                            device_id=to[d], device_id_type=MESH)

    copies = [copy(N_, rs.at[0], rr.at[1]), copy(S_, rs.at[1], rr.at[0]),
              copy(W_, es.at[0], er.at[1]), copy(E_, es.at[1], er.at[0]),
              copy(NW_, ds.at[0, 0], dr.at[1, 1]), copy(NE_, ds.at[1, 0], dr.at[0, 1]),
              copy(SW_, ds.at[0, 1], dr.at[1, 0]), copy(SE_, ds.at[1, 1], dr.at[0, 0])]
    for arr in range(2):
        for j in range(8):
            rs[0, 8 * arr + j] = gl[arr, j, pl.ds(8, 8), :]
            rs[1, 8 * arr + j] = gl[arr, j, pl.ds(512, 8), :]

    index = jnp.where((lane >= 8) & (lane < 72), 16 * ((lane - 8) & 7) + 2 * ((lane - 8) >> 3), 0)

    def cells(grp, js):
        out = []
        for a in range(3):
            op = jnp.maximum if a == 2 else jnp.minimum
            x = tree([ca[a, j, pl.ds(8 * grp, 8), :] for j in js], (8, 4, 2), 1, lane, op)
            x = op(x, pltpu.roll(x, 127, 1))
            out.append(jnp.take_along_axis(x, index, axis=1))
        return out

    def keep(grp, x):
        for a in range(3):
            cp[a, pl.ds(8 * grp, 8), :] = x[a]

    packs = []
    for grp in range(4):
        x = cells(grp, range(8) if grp in (0, 3) else (0, 0, 0, 0, 7, 7, 7, 7))
        if grp in (0, 3):
            keep(grp, x)
            for a in range(3):
                rs[grp // 3, 16 + a] = x[a]
        pk = jnp.where(
            ((lane >= 8) & (lane < 16)) | ((lane >= 64) & (lane < 72)), x[0],
            jnp.where(((lane >= 16) & (lane < 24)) | ((lane >= 72) & (lane < 80)),
                      pltpu.roll(x[1], 8, 1), pltpu.roll(x[2], 16, 1)))
        packs.append(pk)
        for side in range(2):
            if grp in (0, 3):
                ds[side, grp // 3, 1] = pk
    strip = lane & 15

    def ends_at(k):
        return [pl.ds(k, 8, stride=KE), pl.ds(440 + k, 8, stride=KE)]

    def sides_at(k):
        return [pl.ds(72 + 8 * KS * m + k, 8, stride=KS) for m in range(8)]

    def outer(arr, at):
        return jnp.where(lane < 64, gl[arr, 0, at, :], gl[arr, 7, at, :])

    def edges_of(arr, ats):
        t = jnp.concatenate([outer(arr, at) for at in ats], axis=0).T
        return t[0:8, :], t[120:128, :]

    rest = []
    corners = []
    for arr in range(2):
        first8 = edges_of(arr, [at for k in range(8) for at in ends_at(k)])
        rest.append(edges_of(arr, [at for k in range(8, 16) for at in ends_at(min(k, KE - 1))]))
        for side in range(2):
            es[side, arr] = first8[side]
        for p in range(3):
            x = edges_of(arr, sides_at(2 * p) + sides_at(2 * p + 1))
            for side in range(2):
                es[side, 2 + 3 * arr + p] = x[side]
        cb[arr, pl.ds(0, 8, stride=16), :] = outer(arr, pl.ds(512, 8))
        cb[arr, pl.ds(15, 8, stride=16), :] = pltpu.roll(outer(arr, pl.ds(8, 8)), 3, 0)
        t = cb[arr].T
        corners.append((t[0:8, :], t[120:128, :]))
    for side in range(2):
        x = packs[0]
        for t in range(4):
            y = pltpu.roll(packs[t], (24 * t + (24 if side == 0 else 96)) % 128, 1)
            x = jnp.where(lane < 32 + 24 * t, x, y)
        es[side, 8] = x
        es[side, 9] = jnp.where(lane < 48, rest[0][side], pltpu.roll(rest[1][side], 48, 1))
        x = jnp.where((strip == 0) | (strip == 15), corners[0][side], pltpu.roll(corners[1][side], 2, 1))
        ds[side, 0, 0] = x
        ds[side, 1, 0] = x

    def turn(dst, arr, k, ats):
        parts = [gl[arr, j, at, :] for j in range(8) for at in ats]
        dst[arr, k, pl.ds(8, 128), :] = jnp.concatenate(parts, axis=0).T

    def coarse_sweeps(gc, kc, v):
        for _ in range(4):
            h = [jnp.minimum(jnp.minimum(pltpu.roll(x, 1, 1), pltpu.roll(x, 127, 1)), x) for x in v]
            up = [pltpu.roll(x, 1, 0) for x in h]
            down = [pltpu.roll(x, 7, 0) for x in h]
            new = []
            for t in range(6):
                u = jnp.where(sub == 0, up[t - 1], up[t])
                d = jnp.where(sub == 7, down[(t + 1) % 6], down[t])
                m = jnp.minimum(jnp.minimum(u, d), h[t])
                new.append(jnp.minimum(jnp.maximum(gc[t], jnp.minimum(v[t], m + COARSE_STEP)), kc[t]))
            v = new
        turned = jnp.concatenate(v + [v[0]] * 10, axis=0).T
        cf[...] = turned

    def rows_of(row0, n):
        for d in range(n):
            for t in range(10):
                at = pl.ds(8 * t, 8)
                zz[d, at, :] = jnp.take_along_axis(cf[at, :], (row0 >> 4) + d, axis=1)

    def groups_of(n):
        for d in range(n):
            for t in range(2):
                y = zz[d, pl.ds(7 + 8 * t, 8), :]
                for j in range(1, 8):
                    y = jnp.where((lane >> 4) == j, zz[d, pl.ds(7 + 8 * j + 8 * t, 8), :], y)
                yy[d, pl.ds(8 * t, 8), :] = y

    def levels(row0, n, K, tiles):
        for k in range(K):
            e = ((row0 & 15) + k) >> 4
            for t in range(tiles):
                at = pl.ds(8 * t, 8)
                x = yy[n - 1, at, :]
                for d in range(n - 2, -1, -1):
                    x = jnp.where(e == d, yy[d, at, :], x)
                xb[k, at, :] = x

    def begin(tt, v, k):
        for t in range(AJ):
            at = pl.ds(8 * t, 8)
            x = xb[k, pl.ds((t + 1) // 2, 8, stride=0), :]
            v[k + 1, at, :] = jnp.minimum(jnp.maximum(tt[0, k, at, :], x), tt[1, k, at, :])

    def wrap(v, K, A):
        for t in range(A):
            at = pl.ds(8 * t, 8)
            v[0, at, :] = pltpu.roll(v[K, at, :], 1, 1)
            v[K + 1, at, :] = pltpu.roll(v[1, at, :], 127, 1)

    def inside_start():
        for grp in (1, 2):
            arrived(3 + grp)
            groups(grp, 1, 7)
        for grp in (1, 2):
            keep(grp, cells(grp, range(8)))
        near = [[cp[a, pl.ds(8 * min(max(t - 1, 0), 3), 8), :] for t in range(6)] for a in range(3)]
        coarse_sweeps(*near)

        def rows_to_lanes(i, carry):
            for u in range(5):
                k = 5 * i + u
                for arr in range(2):
                    turn(ti, arr, k, [pl.ds(64 + k, 8, stride=KI), pl.ds(264 + k, 8, stride=KI)])
            return carry

        lax.fori_loop(0, KI // 5, rows_to_lanes, 0)
        for arr in range(2):
            for k in range(KI):
                ti[arr, k, pl.ds(0, 8), :] = pltpu.roll(ti[arr, k, pl.ds(128, 8), :], 16, 1)
                ti[arr, k, pl.ds(136, 8), :] = pltpu.roll(ti[arr, k, pl.ds(8, 8), :], 112, 1)
        row0 = 184 + KI * strip
        rows_of(row0, 3)
        groups_of(3)
        levels(row0, 3, KI, 2)

        def start(k, carry):
            begin(ti, vi, k)
            return carry

        lax.fori_loop(0, KI, start, 0)
        wrap(vi, KI, AJ)

    def inside_sweeps():
        def two(i, carry):
            sweep(vi, wi, ti.at[0], KI, AJ, True)
            sweep(wi, vi, ti.at[0], KI, AJ, True)
            return carry

        lax.fori_loop(0, 2, two, 0)

    def inside_end():
        inside_sweeps()

        def back(i, carry):
            for u in range(5):
                k = 5 * i + u
                t = vi[k + 1, pl.ds(8, 128), :].T
                for j in range(8):
                    for h in range(2):
                        ov[j, pl.ds(56 + k + KI * 8 * h, 8, stride=KI), :] = t[16 * j + 8 * h : 16 * j + 8 * h + 8, :]
            return carry

        lax.fori_loop(0, KI // 5, back, 0)

        def ends_to_lanes(k, carry):
            for arr in range(2):
                turn(te, arr, k, ends_at(k))
            return carry

        lax.fori_loop(0, KE, ends_to_lanes, 0, unroll=KE)
        for k in range(KS):
            for arr in range(2):
                t = jnp.concatenate([gl[arr, j, at, :] for j in (0, 7) for at in sides_at(k)], axis=0).T
                for u in range(AS):
                    x = t[8 * u + 48 : 8 * u + 56, :] if u < 10 else None
                    if u:
                        y = t[8 * u - 8 : 8 * u, :]
                        x = y if x is None else jnp.where(lane < 64, y, x)
                    ts[arr, k, pl.ds(8 * u, 8), :] = x

    row, col = lax.axis_index("row"), lax.axis_index("col")
    early = (col == 0) | ((row == 0) & (lax.rem(col, 4) == 1))
    earliest = (row == 0) & (col == 0)

    @pl.when(early)
    def _():
        inside_start()

    @pl.when(earliest)
    def _():
        inside_sweeps()

    pl.semaphore_wait(barrier, 8)
    for i in (W_, E_, NW_, NE_, SW_, SE_, N_, S_):
        copies[i].start()

    @pl.when(jnp.logical_not(early))
    def _():
        inside_start()

    @pl.when(jnp.logical_not(earliest))
    def _():
        inside_sweeps()

    inside_end()

    def result(i):
        if i < 8:
            j, src, at = i, ov.at[i, pl.ds(72, 368), :], pl.ds(72, 368)
        elif i < 16:
            j, src, at = i - 8, oe.at[i - 8, pl.ds(8, 72), :], pl.ds(0, 72)
        else:
            j, src, at = i - 16, oe.at[i - 16, pl.ds(96, 72), :], pl.ds(440, 72)
        return pltpu.make_async_copy(src, o_h.at[at, pl.ds(128 * j, 128)], out_sem.at[i])

    for i in range(1, 7):
        result(i).start()
    for i in range(8):
        copies[i].wait()

    for arr in range(2):
        up = [jnp.where(north, F32(HUGE), rr[0, 8 * arr + j]) for j in range(8)]
        down = [pltpu.roll(jnp.where(south, F32(HUGE), rr[1, 8 * arr + j]), 2, 0) for j in range(8)]
        for odd in range(2):
            parts = []
            for j in range(8):
                parts.append(jnp.where((sub & 1) == odd, up[j], down[(j + 7) % 8]))
                parts.append(down[(j + 7) % 8])
            ht[arr, odd, :, :] = jnp.concatenate(parts, axis=0).T
    for arr in range(2):
        for k in range(KE):
            for i in range(16):
                at = pl.ds(8 + 8 * i, 8)
                h = pltpu.roll(ht[arr, k % 2, pl.ds(8 * i, 8), :], (128 - k) % 128, 1)
                x = te[arr, k, at, :]
                if k < 8:
                    x = jnp.where(strip == 0, h, x)
                if k >= 3:
                    x = jnp.where(strip == 15, h, x)
                te[arr, k, at, :] = x
        edge = []
        for side in range(2):
            up, down = (pltpu.roll(dr[side, i, 0], 126, 1) if arr else dr[side, i, 0] for i in range(2))
            up = jnp.where(north, F32(HUGE), up)
            down = jnp.where(south, F32(HUGE), down)
            e = [er[side, arr], pltpu.roll(er[side, 9], 80, 1) if arr else er[side, 9]]
            e[0] = jnp.where(strip == 0, up, e[0])
            e[0] = jnp.where((strip == 15) & (lane >= 63), down, e[0])
            e[1] = jnp.where((strip == 15) & (lane < 48), down, e[1])
            edge.append(e)
        for k in range(KE):
            own = pltpu.roll(te[arr, k, pl.ds(128, 8), :], 16, 1)
            got = pltpu.roll(edge[0][k // 8], (128 - 16 * (k % 8)) % 128, 1)
            te[arr, k, pl.ds(0, 8), :] = jnp.where(lane < 16, got, own)
            own = pltpu.roll(te[arr, k, pl.ds(8, 8), :], 112, 1)
            got = pltpu.roll(edge[1][k // 8], (112 - 16 * (k % 8)) % 128, 1)
            te[arr, k, pl.ds(136, 8), :] = jnp.where(lane >= 112, got, own)
        for k in range(KS):
            west, east = er[0, 2 + 3 * arr + k // 2], er[1, 2 + 3 * arr + k // 2]
            if k % 2:
                west = pltpu.roll(west, 64, 1)
            else:
                east = pltpu.roll(east, 64, 1)
            ts[arr, k, pl.ds(0, 8), :] = jnp.where(lane < 64, west, ts[arr, k, pl.ds(0, 8), :])
            ts[arr, k, pl.ds(80, 8), :] = jnp.where(lane < 64, ts[arr, k, pl.ds(80, 8), :], east)

    rings = []
    for t in range(6):
        if t in (0, 5):
            west, east = (dr[i, t // 5, 1] for i in range(2))
        else:
            west, east = (pltpu.roll(er[i, 8], (b - 24 * t + 24) % 128, 1) for i, b in ((0, 32), (1, 104)))
        rings.append(jnp.where(lane < 64, east, west))
    ext = []
    for a in range(3):
        tiles = []
        for t in range(6):
            ring = pltpu.roll(rings[t], 64 - 8 * a, 1)
            mid = rr[0, 16 + a] if t == 0 else rr[1, 16 + a] if t == 5 else cp[a, pl.ds(8 * t - 8, 8), :]
            x = jnp.where((lane >= 8) & (lane < 72), mid, ring)
            if t == 0:
                x = jnp.where(north, F32(HUGE), x)
            if t == 5:
                x = jnp.where(south, F32(HUGE), x)
            tiles.append(x)
        ext.append(tiles)
    coarse_sweeps(*ext)
    row0 = jnp.where(strip < 8, 120 + KE * strip, 560 + KE * (strip - 8))
    rows_of(row0, 2)
    groups_of(2)
    levels(row0, 2, KE, 2)
    for k in range(KE):
        begin(te, ve, k)
    wrap(ve, KE, AJ)
    row0 = 192 + KS * (lane & 63)
    rows_of(row0, 2)
    for d in range(2):
        yy[d, pl.ds(0, 8), :] = jnp.where(lane < 64, zz[d, pl.ds(7, 8), :], zz[d, pl.ds(67, 8), :])
    levels(row0, 2, KS, 1)
    for k in range(KS):
        for t in range(AS):
            at = pl.ds(8 * t, 8)
            x = jnp.where(lane < 64, xb[k, pl.ds((t + 1) // 2, 8, stride=0), :], xb[k, pl.ds(t // 2, 8, stride=0), :])
            vs[k + 1, at, :] = jnp.minimum(jnp.maximum(ts[0, k, at, :], x), ts[1, k, at, :])
    wrap(vs, KS, AS)

    def two_outer(i, carry):
        sweep(ve, we, te.at[0], KE, AJ, False)
        sweep(vs, ws, ts.at[0], KS, AS, False)
        sweep(we, ve, te.at[0], KE, AJ, False)
        sweep(ws, vs, ts.at[0], KS, AS, False)
        return carry

    lax.fori_loop(0, 4, two_outer, 0)

    for k in range(KE):
        t = ve[k + 1, pl.ds(8, 128), :].T
        for j in range(8):
            for h in range(2):
                oe[j, pl.ds(k + 88 * h, 8, stride=KE), :] = t[16 * j + 8 * h : 16 * j + 8 * h + 8, :]
    for i in range(8, 24):
        result(i).start()
    for k in range(KS):
        v = [vs[k + 1, pl.ds(8 * u, 8), :] for u in range(AS)]
        tiles = [v[u + 1] if u < 7 else jnp.where(lane < 64, v[u + 1], v[u - 6]) if u < 9 else v[u - 6] for u in range(16)]
        t = jnp.concatenate(tiles, axis=0).T
        for m in range(8):
            at = pl.ds(64 + 8 * KS * m + k, 8, stride=KS)
            ov[0, at, :] = jnp.where(lane < 72, t[8 * m : 8 * m + 8, :], ov[0, at, :])
            ov[7, at, :] = jnp.where(lane >= 56, t[64 + 8 * m : 72 + 8 * m, :], ov[7, at, :])
    result(0).start()
    result(7).start()
    for i in range(24):
        result(i).wait()


def tiled(x):
    return x.reshape(64, 8, 8, 128).transpose(0, 2, 1, 3)


def solution(mesh):
    rows, cols = mesh.shape["row"], mesh.shape["col"]

    def shards(elevation, ocean, outlet):
        scratch = [
            pltpu.VMEM((64, 8, 8, 128), F32),
            pltpu.VMEM((64, 8, 8, 128), jnp.int32),
            pltpu.VMEM((64, 8, 8, 128), jnp.int32),
            pltpu.VMEM((2, 8, 528, 128), F32),
            pltpu.VMEM((2, KI, 144, 128), F32),
            pltpu.VMEM((2, KE, 144, 128), F32),
            pltpu.VMEM((2, KS, 88, 128), F32),
            pltpu.VMEM((KI + 2, 144, 128), F32),
            pltpu.VMEM((KI + 2, 144, 128), F32),
            pltpu.VMEM((KE + 2, 144, 128), F32),
            pltpu.VMEM((KE + 2, 144, 128), F32),
            pltpu.VMEM((KS + 2, 88, 128), F32),
            pltpu.VMEM((KS + 2, 88, 128), F32),
            pltpu.VMEM((8, 512, 128), F32),
            pltpu.VMEM((8, 176, 128), F32),
            pltpu.VMEM((3, 8, 32, 128), F32),
            pltpu.VMEM((3, 32, 128), F32),
            pltpu.VMEM((128, 128), F32),
            pltpu.VMEM((4, 80, 128), F32),
            pltpu.VMEM((4, 16, 128), F32),
            pltpu.VMEM((KI, 16, 128), F32),
            pltpu.VMEM((2, 128, 128), F32),
            pltpu.VMEM((2, 19, 8, 128), F32),
            pltpu.VMEM((2, 19, 8, 128), F32),
            pltpu.VMEM((2, 10, 8, 128), F32),
            pltpu.VMEM((2, 10, 8, 128), F32),
            pltpu.VMEM((2, 2, 2, 8, 128), F32),
            pltpu.VMEM((2, 2, 2, 8, 128), F32),
            pltpu.VMEM((2, 2, 128, 128), F32),
            pltpu.SemaphoreType.DMA((6, 3)),
            pltpu.SemaphoreType.DMA((24,)),
            pltpu.SemaphoreType.DMA((8,)),
            pltpu.SemaphoreType.DMA((8,)),
        ]
        return pl.pallas_call(
            lambda *refs: kernel(rows, cols, *refs),
            out_shape=jax.ShapeDtypeStruct((512, 1024), F32),
            in_specs=[pl.BlockSpec(memory_space=pl.ANY)] * 3,
            out_specs=pl.BlockSpec(memory_space=pl.ANY),
            scratch_shapes=scratch,
            name="fill",
            compiler_params=pltpu.CompilerParams(
                collective_id=0, has_side_effects=True, vmem_limit_bytes=50 << 20
            ),
        )(tiled(elevation), tiled(ocean), tiled(outlet))

    return jax.shard_map(
        shards,
        mesh=mesh,
        in_specs=(P("row", "col"), P("row", "col"), P("row", "col")),
        out_specs=P("row", "col"),
        check_vma=False,
    )
```

time: 23.3 us -> 20.2 us (0.87)
  Pallas kernels: 21.8 us -> 18.8 us
    pallas_call x1, Pallas kernels: 21.8 us -> 18.8 us  [shards(): pl.pallas_call(lambda *refs: kernel(rows, cols, *refs), out_shape=jax.Sha...]
where the time goes in v3:
time: 20.2 us; the launch traced here: 20.1 us
  Pallas kernels  18.8 us (93%)
  local copies, waits for them, and re-layouts  1.32 us (7%)
    pallas_call x1, Pallas kernels, shards(): pl.pallas_call(lambda *refs: kernel(rows, cols, *refs), out_shape=jax.Sha...  18.8 us
    unnamed x1, local copies, waits for them, and re-layouts  1.32 us

profile of v3, /device:TPU:0, one launch (start us, length us, event | category | flops | bytes accessed | tf_op | source)
XLA Modules:
  0.0 20.1 jit_solution(10457204936001223832)
XLA Ops:
  0.0 18.8 %fill.1 = f32[512,1024]{1,0:T(8,128)S(1)} custom-call(f32[64,8,8,128]{3,2,1,0:T(8,128)} %bitcast.9, s32[64,8,8,128]{3,2,1,0:T(8,128)} %bitcast.10, s32[64,8,8,128]{3,2,1,0:T(8,128)} %bitcast.11), custom_call_target="tpu_custom_call" | custom-call | tf_op jit(solution)/shard_map/fill/pallas_call | solution.py:581
  18.8 1.3 %copy.5 = f32[512,1024]{1,0:T(8,128)} copy(f32[512,1024]{1,0:T(8,128)S(1)} %fill.1) | data formatting | bytes 4194304

commit v4 on v3

--- a/solution.py
+++ b/solution.py
@@ -419,6 +419,31 @@
     for i in range(8):
         copies[i].wait()
 
+    rings = []
+    for t in range(6):
+        if t in (0, 5):
+            west, east = (dr[i, t // 5, 1] for i in range(2))
+        else:
+            west, east = (pltpu.roll(er[i, 8], (b - 24 * t + 24) % 128, 1) for i, b in ((0, 32), (1, 104)))
+        rings.append(jnp.where(lane < 64, east, west))
+    ext = []
+    for a in range(3):
+        tiles = []
+        for t in range(6):
+            ring = pltpu.roll(rings[t], 64 - 8 * a, 1)
+            mid = rr[0, 16 + a] if t == 0 else rr[1, 16 + a] if t == 5 else cp[a, pl.ds(8 * t - 8, 8), :]
+            x = jnp.where((lane >= 8) & (lane < 72), mid, ring)
+            if t == 0:
+                x = jnp.where(north, F32(HUGE), x)
+            if t == 5:
+                x = jnp.where(south, F32(HUGE), x)
+            tiles.append(x)
+        ext.append(tiles)
+    coarse_sweeps(*ext)
+    row0 = jnp.where(strip < 8, 120 + KE * strip, 560 + KE * (strip - 8))
+    rows_of(row0, 2)
+    groups_of(2)
+    levels(row0, 2, KE, 2)
     for arr in range(2):
         up = [jnp.where(north, F32(HUGE), rr[0, 8 * arr + j]) for j in range(8)]
         down = [pltpu.roll(jnp.where(south, F32(HUGE), rr[1, 8 * arr + j]), 2, 0) for j in range(8)]
@@ -465,31 +490,6 @@
             ts[arr, k, pl.ds(0, 8), :] = jnp.where(lane < 64, west, ts[arr, k, pl.ds(0, 8), :])
             ts[arr, k, pl.ds(80, 8), :] = jnp.where(lane < 64, ts[arr, k, pl.ds(80, 8), :], east)
 
-    rings = []
-    for t in range(6):
-        if t in (0, 5):
-            west, east = (dr[i, t // 5, 1] for i in range(2))
-        else:
-            west, east = (pltpu.roll(er[i, 8], (b - 24 * t + 24) % 128, 1) for i, b in ((0, 32), (1, 104)))
-        rings.append(jnp.where(lane < 64, east, west))
-    ext = []
-    for a in range(3):
-        tiles = []
-        for t in range(6):
-            ring = pltpu.roll(rings[t], 64 - 8 * a, 1)
-            mid = rr[0, 16 + a] if t == 0 else rr[1, 16 + a] if t == 5 else cp[a, pl.ds(8 * t - 8, 8), :]
-            x = jnp.where((lane >= 8) & (lane < 72), mid, ring)
-            if t == 0:
-                x = jnp.where(north, F32(HUGE), x)
-            if t == 5:
-                x = jnp.where(south, F32(HUGE), x)
-            tiles.append(x)
-        ext.append(tiles)
-    coarse_sweeps(*ext)
-    row0 = jnp.where(strip < 8, 120 + KE * strip, 560 + KE * (strip - 8))
-    rows_of(row0, 2)
-    groups_of(2)
-    levels(row0, 2, KE, 2)
     for k in range(KE):
         begin(te, ve, k)
     wrap(ve, KE, AJ)

time: 20.2 us -> 20.1 us (level)
  no operation moved by 1% of the time
where the time goes in v4:
time: 20.1 us; the launch traced here: 20 us
  Pallas kernels  18.6 us (93%)
  local copies, waits for them, and re-layouts  1.32 us (7%)
    pallas_call x1, Pallas kernels, shards(): pl.pallas_call(lambda *refs: kernel(rows, cols, *refs), out_shape=jax.Sha...  18.6 us
    unnamed x1, local copies, waits for them, and re-layouts  1.32 us

profile of v4, /device:TPU:0, one launch (start us, length us, event | category | flops | bytes accessed | tf_op | source)
XLA Modules:
  0.0 20.0 jit_solution(14070968099158939472)
XLA Ops:
  0.0 18.6 %fill.1 = f32[512,1024]{1,0:T(8,128)S(1)} custom-call(f32[64,8,8,128]{3,2,1,0:T(8,128)} %bitcast.9, s32[64,8,8,128]{3,2,1,0:T(8,128)} %bitcast.10, s32[64,8,8,128]{3,2,1,0:T(8,128)} %bitcast.11), custom_call_target="tpu_custom_call" | custom-call | tf_op jit(solution)/shard_map/fill/pallas_call | solution.py:581
  18.6 1.3 %copy.5 = f32[512,1024]{1,0:T(8,128)} copy(f32[512,1024]{1,0:T(8,128)S(1)} %fill.1) | data formatting | bytes 4194304

commit v5 on v4

--- a/solution.py
+++ b/solution.py
@@ -114,14 +114,14 @@
     for i in (NW_, NE_, SW_, SE_, W_, E_, N_, S_):
         pl.semaphore_signal(barrier, inc=1, device_id=to[i], device_id_type=MESH)
 
-    pieces = [((0, 16), (0, 8)), ((48, 16), (0, 8)), ((16, 32), (0, 1)), ((16, 32), (7, 1)), ((16, 16), (1, 6)), ((32, 16), (1, 6))]
+    pieces = [((0, 16), (0, 4)), ((0, 16), (4, 4)), ((48, 16), (0, 4)), ((48, 16), (4, 4)), ((16, 32), (0, 1)), ((16, 32), (7, 1)), ((16, 16), (1, 6)), ((32, 16), (1, 6))]
 
     def loads(p):
         (r, nr), (j, nj) = pieces[p]
         return [pltpu.make_async_copy(h.at[pl.ds(r, nr), pl.ds(j, nj)], v.at[pl.ds(r, nr), pl.ds(j, nj)], in_sem.at[p, i])
                 for i, (h, v) in enumerate(((e_h, ev), (oc_h, ocv), (ou_h, ouv)))]
 
-    for p in range(6):
+    for p in range(8):
         for c in loads(p):
             c.start()
 
@@ -159,11 +159,10 @@
 
         lax.fori_loop(lo, hi, body, 0, unroll=2)
 
-    arrived(0)
-    groups(0, 0, 8)
-    arrived(1)
-    groups(3, 0, 8)
-    for j, p in ((0, 2), (7, 3)):
+    for p in range(4):
+        arrived(p)
+        groups(3 * (p // 2), 4 * (p % 2), 4 * (p % 2) + 4)
+    for j, p in ((0, 4), (7, 5)):
         arrived(p)
         group(1, j)
         group(2, j)
@@ -310,7 +309,7 @@
 
     def inside_start():
         for grp in (1, 2):
-            arrived(3 + grp)
+            arrived(5 + grp)
             groups(grp, 1, 7)
         for grp in (1, 2):
             keep(grp, cells(grp, range(8)))
@@ -573,7 +572,7 @@
             pltpu.VMEM((2, 2, 2, 8, 128), F32),
             pltpu.VMEM((2, 2, 2, 8, 128), F32),
             pltpu.VMEM((2, 2, 128, 128), F32),
-            pltpu.SemaphoreType.DMA((6, 3)),
+            pltpu.SemaphoreType.DMA((8, 3)),
             pltpu.SemaphoreType.DMA((24,)),
             pltpu.SemaphoreType.DMA((8,)),
             pltpu.SemaphoreType.DMA((8,)),

time: 20.1 us -> 20.2 us (level)
  no operation moved by 1% of the time
where the time goes in v5:
time: 20.2 us; the launch traced here: 20.1 us
  Pallas kernels  18.8 us (93%)
  local copies, waits for them, and re-layouts  1.32 us (7%)
    pallas_call x1, Pallas kernels, shards(): pl.pallas_call(lambda *refs: kernel(rows, cols, *refs), out_shape=jax.Sha...  18.8 us
    unnamed x1, local copies, waits for them, and re-layouts  1.32 us

profile of v5, /device:TPU:0, one launch (start us, length us, event | category | flops | bytes accessed | tf_op | source)
XLA Modules:
  0.0 20.1 jit_solution(10199855355131448939)
XLA Ops:
  0.0 18.8 %fill.1 = f32[512,1024]{1,0:T(8,128)S(1)} custom-call(f32[64,8,8,128]{3,2,1,0:T(8,128)} %bitcast.9, s32[64,8,8,128]{3,2,1,0:T(8,128)} %bitcast.10, s32[64,8,8,128]{3,2,1,0:T(8,128)} %bitcast.11), custom_call_target="tpu_custom_call" | custom-call | tf_op jit(solution)/shard_map/fill/pallas_call | solution.py:580
  18.8 1.3 %copy.5 = f32[512,1024]{1,0:T(8,128)} copy(f32[512,1024]{1,0:T(8,128)S(1)} %fill.1) | data formatting | bytes 4194304
